TPU v7x, 256 devices: a whole 4x4x8 slice. The times are simulated.
256 devices in a mesh: section: 8 (over y, core), ctx: 32 (over z, x).
Axes of the slice: x: 4, y: 4, z: 8, core: 2. Of those that a mesh axis runs over, the one named last changes fastest.
Arguments:
- section_input: bfloat16 [2, 4096, 2048], P(None, 'ctx'), may hold values from -6 to 6
- cotangent: bfloat16 [2, 4096, 2048], P(None, 'ctx'), may hold values from -6 to 6
- w_query: bfloat16 [8, 2048, 1024], P('section', 'ctx'), may hold values from -0.125 to 0.125
- w_key: bfloat16 [8, 2048, 1024], P('section', 'ctx'), may hold values from -0.125 to 0.125
- w_value: bfloat16 [8, 2048, 1024], P('section', 'ctx'), may hold values from -0.125 to 0.125
- w_out: bfloat16 [8, 1024, 2048], P('section', 'ctx'), may hold values from -0.1875 to 0.1875
- block_mask: int32 [2, 128, 2], P(None, 'ctx'), may hold values 0 or 1
Outputs:
- section_output: bfloat16 [8, 2, 4096, 2048], P('section', None, 'ctx')
- input_grad: bfloat16 [8, 2, 4096, 2048], P('section', None, 'ctx')
Inputs may be any that keep to these rules, and one draw needn't show every extreme that they name: A block always attends to itself; column 0 and 1 of block_mask choose its two neighbour blocks.
All inputs are finite; a program needn't handle non-finite values.
Results may differ from a plain program's by a relative error of at most 0.03.
Values may be sent and summed in bfloat16 or wider, within the bound.
No kernel may reach another device: no remote copies, remote signals or barrier semaphores. Data moves between devices by JAX's collectives and lax.ppermute only.
A program may use at most 128 MiB of HBM per device.

v0:
```python
import jax
import jax.numpy as jnp
from jax import lax
from jax.sharding import PartitionSpec as P

D = 2048
HEADS = 8
HDIM = 128
BLOCKS_DEV = 4
BLK = 32


def padded(block, sides, width):
    for axis, dim in sides:
        count = lax.axis_size(axis)
        forward = [(i, i + 1) for i in range(count - 1)]
        backward = [(target, source) for source, target in forward]
        low = lax.ppermute(
            lax.slice_in_dim(block, block.shape[dim] - width, None, axis=dim), axis, forward
        )
        high = lax.ppermute(lax.slice_in_dim(block, 0, width, axis=dim), axis, backward)
        block = jnp.concatenate([low, block, high], axis=dim)
    return block


def shifted(block, axis, distance):
    devices = range(lax.axis_size(axis))
    route = [(i - distance, i) for i in devices if i - distance in devices]
    return lax.ppermute(block, axis, route)


def rms_scale(values):
    return values * lax.rsqrt(jnp.mean(values * values, axis=-1, keepdims=True) + 1e-06)


def allowed_keys(mask_rows, block_ids, block_count):
    mask_float = mask_rows.astype(jnp.float32)
    left = mask_float[:, 0] * (block_ids > 0).astype(jnp.float32)
    right = mask_float[:, 1] * (block_ids < block_count - 1).astype(jnp.float32)
    return jnp.stack([left, jnp.ones_like(left), right], axis=1)


def project(layer_in, w_query, w_key, w_value):
    length = layer_in.shape[0]
    normed = rms_scale(layer_in.astype(jnp.float32)).astype(jnp.bfloat16)

    def head_normed(weight):
        out = jnp.dot(normed, weight, preferred_element_type=jnp.float32)
        out = rms_scale(out.reshape(length, HEADS, HDIM))
        return out.reshape(length, HEADS * HDIM).astype(jnp.bfloat16)

    query = head_normed(w_query)
    key = head_normed(w_key)
    value = jnp.dot(normed, w_value, preferred_element_type=jnp.float32).astype(jnp.bfloat16)
    return (query, key, value)


def attend(query, keys_ext, values_ext, allow, layer_in, w_out):
    length = query.shape[0]
    nblock = length // BLK
    queries = query.reshape(nblock, BLK, HEADS, HDIM)

    def windows(extended):
        grid = extended.reshape(nblock + 2, BLK, HEADS, HDIM)
        return jnp.concatenate([grid[:-2], grid[1:-1], grid[2:]], axis=1)

    keys = windows(keys_ext)
    values = windows(values_ext)
    scores = jnp.einsum(
        "bqhd,bkhd->bhqk", queries, keys, preferred_element_type=jnp.float32
    ) * HDIM ** (-0.5)
    weight = jnp.repeat(allow, BLK, axis=1)[:, None, None, :]
    probs = jnp.exp(scores) * weight
    total = jnp.sum(probs, axis=-1)
    attended = jnp.einsum(
        "bhqk,bkhd->bqhd", probs.astype(jnp.bfloat16), values, preferred_element_type=jnp.float32
    )
    attended = attended / jnp.transpose(total, (0, 2, 1))[..., None]
    attended = attended.reshape(length, HEADS * HDIM).astype(jnp.bfloat16)
    update = jnp.dot(attended, w_out, preferred_element_type=jnp.float32)
    return (layer_in.astype(jnp.float32) + update).astype(jnp.bfloat16)


def put_slot(buffer, value, slot, active):
    return jnp.where(active, lax.dynamic_update_index_in_dim(buffer, value, slot, 0), buffer)


def take_slot(buffer, slot):
    return lax.dynamic_index_in_dim(buffer, slot, 0, keepdims=False)


def per_device(section_input, cotangent, w_query, w_key, w_value, w_out, block_mask):
    n_section = lax.axis_size("section")
    n_ctx = lax.axis_size("ctx")
    section = lax.axis_index("section")
    place = lax.axis_index("ctx")
    micro = section_input.shape[0]
    length = section_input.shape[1]
    width = HEADS * HDIM
    full_query, full_key, full_value, full_out = (
        lax.all_gather(w_query[0], "ctx", axis=0, tiled=True),
        lax.all_gather(w_key[0], "ctx", axis=0, tiled=True),
        lax.all_gather(w_value[0], "ctx", axis=0, tiled=True),
        lax.all_gather(w_out[0], "ctx", axis=0, tiled=True),
    )
    block_ids = place * BLOCKS_DEV + jnp.arange(BLOCKS_DEV)
    allows = jax.vmap(lambda rows_mask: allowed_keys(rows_mask, block_ids, BLOCKS_DEV * n_ctx))(
        block_mask
    )
    zero_rows = jnp.zeros((length, D), jnp.bfloat16)
    zero_heads = jnp.zeros((length, width), jnp.bfloat16)
    zero_wide = jnp.zeros((length + 2 * BLK, width), jnp.bfloat16)
    steps_total = n_section + micro - 1

    def run_project(values):
        return project(values, full_query, full_key, full_value)

    def skip_project(values):
        return (zero_heads, zero_heads, zero_heads)

    def run_attend(query, extended, layer_in, allow):
        return attend(query, extended[0], extended[1], allow, layer_in, full_out)

    def skip_attend(query, extended, layer_in, allow):
        return zero_rows

    kv_store = jnp.zeros((micro, 2, length, width), jnp.bfloat16)
    inputs = jnp.zeros((micro, length, D), jnp.bfloat16)
    outputs = jnp.zeros((micro, length, D), jnp.bfloat16)
    queries = jnp.zeros((micro, length, width), jnp.bfloat16)

    def forward_step(step, carry):
        incoming, inputs, outputs, queries, kv_store = carry
        micro_id = step - section
        active = (micro_id >= 0) & (micro_id < micro)
        slot = jnp.clip(micro_id, 0, micro - 1)
        layer_in = jnp.where(section == 0, take_slot(section_input, slot), incoming)
        query, key, value = lax.cond(active, run_project, skip_project, layer_in)
        local_kv = jnp.stack([key, value])
        extended = padded(local_kv, (("ctx", 1),), BLK)
        allow = take_slot(allows, slot)
        result = lax.cond(active, run_attend, skip_attend, query, extended, layer_in, allow)
        inputs = put_slot(inputs, layer_in, slot, active)
        outputs = put_slot(outputs, result, slot, active)
        queries = put_slot(queries, query, slot, active)
        kv_store = put_slot(kv_store, local_kv, slot, active)
        incoming = shifted(result, "section", 1)
        return (incoming, inputs, outputs, queries, kv_store)

    carry = (zero_rows, inputs, outputs, queries, kv_store)
    _, inputs, outputs, queries, kv_store = lax.fori_loop(0, steps_total, forward_step, carry)

    def pull_attend(query, extended, layer_in, allow, grad_in):

        def local_attend(query_in, keys_in, values_in, rows_in):
            return attend(query_in, keys_in, values_in, allow, rows_in, full_out)

        _, pull = jax.vjp(local_attend, query, extended[0], extended[1], layer_in)
        return pull(grad_in)

    def skip_pull(query, extended, layer_in, allow, grad_in):
        return (zero_heads, zero_wide, zero_wide, zero_rows)

    def pull_project(layer_in, d_query, own):
        _, pull = jax.vjp(run_project, layer_in)
        return pull((d_query, own[0], own[1]))[0]

    def skip_pull_project(layer_in, d_query, own):
        return zero_rows

    grads = jnp.zeros((micro, length, D), jnp.bfloat16)

    def backward_step(step, carry):
        incoming, grads = carry
        micro_id = step - (n_section - 1 - section)
        active = (micro_id >= 0) & (micro_id < micro)
        slot = jnp.clip(micro_id, 0, micro - 1)
        grad_in = jnp.where(section == n_section - 1, take_slot(cotangent, slot), incoming)
        layer_in = take_slot(inputs, slot)
        query = take_slot(queries, slot)
        extended = padded(take_slot(kv_store, slot), (("ctx", 1),), BLK)
        allow = take_slot(allows, slot)
        d_query, d_keys, d_values, d_direct = lax.cond(
            active, pull_attend, skip_pull, query, extended, layer_in, allow, grad_in
        )
        d_wide = jnp.stack([d_keys, d_values])
        rims = jnp.concatenate([d_wide[:, :BLK], d_wide[:, -BLK:]], axis=1)
        returned = padded(rims, (("ctx", 1),), BLK)
        own = d_wide[:, BLK:-BLK]
        own = own.at[:, :BLK].add(returned[:, :BLK])
        own = own.at[:, -BLK:].add(returned[:, -BLK:])
        d_projected = lax.cond(active, pull_project, skip_pull_project, layer_in, d_query, own)
        d_input = d_direct + d_projected
        grads = put_slot(grads, d_input, slot, active)
        incoming = shifted(d_input, "section", -1)
        return (incoming, grads)

    _, grads = lax.fori_loop(0, steps_total, backward_step, (zero_rows, grads))
    return (outputs[None], grads[None])


def solution(mesh):
    return jax.shard_map(
        per_device,
        mesh=mesh,
        in_specs=(
            P(None, "ctx", None),
            P(None, "ctx", None),
            P("section", "ctx", None),
            P("section", "ctx", None),
            P("section", "ctx", None),
            P("section", "ctx", None),
            P(None, "ctx", None),
        ),
        out_specs=(P("section", None, "ctx", None), P("section", None, "ctx", None)),
        check_vma=False,
    )
```

profile of v0, /device:TPU:103, one launch (start us, length us, event | category | flops | bytes accessed | tf_op | source)
XLA Modules:
  0.0 1315.3 jit_solution(2852460559565105699)
XLA Ops:
  11.0 78.0 %all-gather.9.cloned.1.call-done = bf16[1,2048,1024]{2,1,0:T(8,128)(2,1)} async-done(((bf16[1,64,1024]{2,1,0:T(8,128)(2,1)}), bf16[1,2048,1024]{2,1,0:T(8,128)(2,1)}) %all-gather.9.cloned.1.call-update) | async-done | bytes 4194320 | tf_op jit(solution)/shard_map/all_gather | solution.py:101
  88.9 81.8 %all-gather.11.cloned.1.call-done = bf16[1,2048,1024]{2,1,0:T(8,128)(2,1)} async-done(((bf16[1,64,1024]{2,1,0:T(8,128)(2,1)}), bf16[1,2048,1024]{2,1,0:T(8,128)(2,1)}) %all-gather.11.cloned.1.call-update) | async-done | bytes 4194320 | tf_op jit(solution)/shard_map/all_gather | solution.py:102
  170.7 81.8 %all-gather.13.cloned.1.call-done = bf16[1,2048,1024]{2,1,0:T(8,128)(2,1)} async-done(((bf16[1,64,1024]{2,1,0:T(8,128)(2,1)}), bf16[1,2048,1024]{2,1,0:T(8,128)(2,1)}) %all-gather.13.cloned.1.call-update) | async-done | bytes 4194320 | tf_op jit(solution)/shard_map/all_gather | solution.py:103
  252.5 81.6 %all-gather.15.cloned.1.call-done = bf16[1,1024,2048]{2,1,0:T(8,128)(2,1)} async-done(((bf16[1,32,2048]{2,1,0:T(8,128)(2,1)}), bf16[1,1024,2048]{2,1,0:T(8,128)(2,1)}) %all-gather.15.cloned.1.call-update) | async-done | bytes 4194320 | tf_op jit(solution)/shard_map/all_gather | solution.py:104
  337.4 301.7 %while.41 = (s32[]{:T(128)}, bf16[128,2048]{1,0:T(8,128)(2,1)S(1)}, bf16[2,128,2048]{2,1,0:T(8,128)(2,1)S(1)}, bf16[2,128,2048]{2,1,0:T(8,128)(2,1)}, bf16[2,128...) while((s32[]{:T(128)}, bf16[128,2048]{1,0:T(8,128)(2,1)S(1)}, ...), condition=%wide.region_9.10_spmd, body=%wide.region_0.9_spmd.sunk | while | flops 2211841024 | bytes 75189416 | solution.py:151
  362.1 12.5 collective-permute-done.2
  376.0 10.8 conditional.8
  414.6 10.8 conditional.8
  468.4 21.3 %collective-permute-start.2 = (bf16[128,2048]{1,0:T(8,128)(2,1)}, bf16[128,2048]{1,0:T(8,128)(2,1)S(1)}, u32[]{:S(2)}, u32[]{:S(2)}) collective-permute-start(bf16[128,2048]{1,0:T(8,128)(2,1)} %get-tuple-element.1251), channel_id=1, source_target_pairs={{0,32},{32,64},{64,96},{96,128},{128,160},{160,192},{192,224},{1,3... | collective-permute-start | bytes 1572872 | tf_op jit(solution)/shard_map/while/body/eval_jaxpr/ppermute | solution.py:29
  589.5 17.8 %collective-permute-start.2 = (bf16[128,2048]{1,0:T(8,128)(2,1)}, bf16[128,2048]{1,0:T(8,128)(2,1)S(1)}, u32[]{:S(2)}, u32[]{:S(2)}) collective-permute-start(bf16[128,2048]{1,0:T(8,128)(2,1)} %get-tuple-element.1251), channel_id=1, source_target_pairs={{0,32},{32,64},{64,96},{96,128},{128,160},{160,192},{192,224},{1,3... | collective-permute-start | bytes 1572872 | tf_op jit(solution)/shard_map/while/body/eval_jaxpr/ppermute | solution.py:29
  641.0 667.8 %while.42 = (s32[]{:T(128)}, bf16[128,2048]{1,0:T(8,128)(2,1)}, bf16[2,128,2048]{2,1,0:T(8,128)(2,1)}, s32[]{:T(128)}, bf16[2,2,128,1024]{3,2,1,0:T(8,128)(2,1)}...) while((s32[]{:T(128)}, bf16[128,2048]{1,0:T(8,128)(2,1)}, ...), condition=%wide.region_24.25_spmd, body=%wide.region_10.24_spmd.sunk | while | flops 3389073152 | bytes 170649296 | solution.py:198
  675.7 15.2 %collective-permute-done.7 = bf16[128,2048]{1,0:T(8,128)(2,1)S(1)} collective-permute-done((bf16[128,2048]{1,0:T(8,128)(2,1)S(1)}, bf16[128,2048]{1,0:T(8,128)(2,1)S(1)}, u32[]{:S(2)}, u32[]{:S(2)}) %collective-permute-start.7) | collective-permute-done | bytes 524320 | tf_op jit(solution)/shard_map/while/body/eval_jaxpr/ppermute | solution.py:29
  726.8 9.4 collective-permute-done.7
  771.0 22.7 %collective-permute-done.7 = bf16[128,2048]{1,0:T(8,128)(2,1)S(1)} collective-permute-done((bf16[128,2048]{1,0:T(8,128)(2,1)S(1)}, bf16[128,2048]{1,0:T(8,128)(2,1)S(1)}, u32[]{:S(2)}, u32[]{:S(2)}) %collective-permute-start.7) | collective-permute-done | bytes 524320 | tf_op jit(solution)/shard_map/while/body/eval_jaxpr/ppermute | solution.py:29
  828.4 9.2 collective-permute-done.7
  872.5 14.1 %collective-permute-done.7 = bf16[128,2048]{1,0:T(8,128)(2,1)S(1)} collective-permute-done((bf16[128,2048]{1,0:T(8,128)(2,1)S(1)}, bf16[128,2048]{1,0:T(8,128)(2,1)S(1)}, u32[]{:S(2)}, u32[]{:S(2)}) %collective-permute-start.7) | collective-permute-done | bytes 524320 | tf_op jit(solution)/shard_map/while/body/eval_jaxpr/ppermute | solution.py:29
  922.3 176.7 %collective-permute-done.7 = bf16[128,2048]{1,0:T(8,128)(2,1)S(1)} collective-permute-done((bf16[128,2048]{1,0:T(8,128)(2,1)S(1)}, bf16[128,2048]{1,0:T(8,128)(2,1)S(1)}, u32[]{:S(2)}, u32[]{:S(2)}) %collective-permute-start.7) | collective-permute-done | bytes 524320 | tf_op jit(solution)/shard_map/while/body/eval_jaxpr/ppermute | solution.py:29
  1111.5 11.2 conditional.10
  1140.7 18.6 %conditional.11 = (bf16[128,2048]{1,0:T(8,128)(2,1)S(1)}) conditional(s32[]{:T(128)} %convert_element_type.302, () %tuple.209, (bf16[2,192,1024]{2,1,0:T(8,128)(2,1)S(1)}, bf16[2,32,1024]{2,1,0:T(8,128)(2,1)S(1)}, bf16[2,32,1024]{2,1,0:T(8,128)(2,1)S(1)}, bf16[2048,1024]{1,0:T(8,128)(2,1)}, bf16[2,128,2048]{2,1,0:T(8,128)(2,1)S(1)}, ...), branch_computations={%region_15.15_spmd, %region_16.23_spmd} | conditional | flops 2693800704 | bytes 90314520 | solution.py:192
  1163.4 9.5 collective-permute-done.7
  1185.4 11.2 conditional.10
  1214.6 18.6 %conditional.11 = (bf16[128,2048]{1,0:T(8,128)(2,1)S(1)}) conditional(s32[]{:T(128)} %convert_element_type.302, () %tuple.209, (bf16[2,192,1024]{2,1,0:T(8,128)(2,1)S(1)}, bf16[2,32,1024]{2,1,0:T(8,128)(2,1)S(1)}, bf16[2,32,1024]{2,1,0:T(8,128)(2,1)S(1)}, bf16[2048,1024]{1,0:T(8,128)(2,1)}, bf16[2,128,2048]{2,1,0:T(8,128)(2,1)S(1)}, ...), branch_computations={%region_15.15_spmd, %region_16.23_spmd} | conditional | flops 2693800704 | bytes 90314520 | solution.py:192
  1237.4 8.6 collective-permute-done.7
  1278.8 27.7 %collective-permute-start.7 = (bf16[128,2048]{1,0:T(8,128)(2,1)S(1)}, bf16[128,2048]{1,0:T(8,128)(2,1)S(1)}, u32[]{:S(2)}, u32[]{:S(2)}) collective-permute-start(bf16[128,2048]{1,0:T(8,128)(2,1)S(1)} %get-tuple-element.1276), channel_id=1, source_target_pairs={{32,0},{64,32},{96,64},{128,96},{160,128},{192,160},{224,192},{33,... | collective-permute-start | bytes 1572872 | tf_op jit(solution)/shard_map/while/body/eval_jaxpr/ppermute | solution.py:29
  (720 shorter events, 651.3 us)
Async XLA Ops:
  7.2 81.8 %all-gather.9.cloned.1.call-start = ((), (), s32[]{:S(2)}) async-start(), calls=%async_computation | async-start | bytes 4325376 | tf_op jit(solution)/shard_map/all_gather | solution.py:101
  7.9 162.8 %all-gather.11.cloned.1.call-start = ((), (), s32[]{:S(2)}) async-start(), calls=%async_computation.1 | async-start | bytes 4325376 | tf_op jit(solution)/shard_map/all_gather | solution.py:102
  8.6 243.8 %all-gather.13.cloned.1.call-start = ((), (), s32[]{:S(2)}) async-start(), calls=%async_computation.2 | async-start | bytes 4325376 | tf_op jit(solution)/shard_map/all_gather | solution.py:103
  9.4 324.7 %all-gather.15.cloned.1.call-start = ((), (), s32[]{:S(2)}) async-start(), calls=%async_computation.3 | async-start | bytes 4325376 | tf_op jit(solution)/shard_map/all_gather | solution.py:104
  350.6 24.1 %collective-permute-start.2 = (bf16[128,2048]{1,0:T(8,128)(2,1)}, bf16[128,2048]{1,0:T(8,128)(2,1)S(1)}, u32[]{:S(2)}, u32[]{:S(2)}) collective-permute-start(bf16[128,2048]{1,0:T(8,128)(2,1)} %get-tuple-element.1251), channel_id=1, source_target_pairs={{0,32},{32,64},{64,96},{96,128},{128,160},{160,192},{192,224},{1,3... | collective-permute-start | bytes 1572872 | tf_op jit(solution)/shard_map/while/body/eval_jaxpr/ppermute | solution.py:29
  443.1 11.4 collective-permute-start.2
  456.0 11.4 collective-permute-start
  468.4 27.8 %collective-permute-start.2 = (bf16[128,2048]{1,0:T(8,128)(2,1)}, bf16[128,2048]{1,0:T(8,128)(2,1)S(1)}, u32[]{:S(2)}, u32[]{:S(2)}) collective-permute-start(bf16[128,2048]{1,0:T(8,128)(2,1)} %get-tuple-element.1251), channel_id=1, source_target_pairs={{0,32},{32,64},{64,96},{96,128},{128,160},{160,192},{192,224},{1,3... | collective-permute-start | bytes 1572872 | tf_op jit(solution)/shard_map/while/body/eval_jaxpr/ppermute | solution.py:29
  497.7 11.4 collective-permute-start
  510.1 11.4 collective-permute-start.2
  523.0 11.4 collective-permute-start
  535.4 14.8 %collective-permute-start.2 = (bf16[128,2048]{1,0:T(8,128)(2,1)}, bf16[128,2048]{1,0:T(8,128)(2,1)S(1)}, u32[]{:S(2)}, u32[]{:S(2)}) collective-permute-start(bf16[128,2048]{1,0:T(8,128)(2,1)} %get-tuple-element.1251), channel_id=1, source_target_pairs={{0,32},{32,64},{64,96},{96,128},{128,160},{160,192},{192,224},{1,3... | collective-permute-start | bytes 1572872 | tf_op jit(solution)/shard_map/while/body/eval_jaxpr/ppermute | solution.py:29
  551.8 11.4 collective-permute-start
  564.2 11.4 collective-permute-start.2
  577.1 11.4 collective-permute-start
  589.5 24.3 %collective-permute-start.2 = (bf16[128,2048]{1,0:T(8,128)(2,1)}, bf16[128,2048]{1,0:T(8,128)(2,1)S(1)}, u32[]{:S(2)}, u32[]{:S(2)}) collective-permute-start(bf16[128,2048]{1,0:T(8,128)(2,1)} %get-tuple-element.1251), channel_id=1, source_target_pairs={{0,32},{32,64},{64,96},{96,128},{128,160},{160,192},{192,224},{1,3... | collective-permute-start | bytes 1572872 | tf_op jit(solution)/shard_map/while/body/eval_jaxpr/ppermute | solution.py:29
  615.3 11.4 collective-permute-start
  627.7 11.4 collective-permute-start.2
  673.8 17.1 %collective-permute-start.7 = (bf16[128,2048]{1,0:T(8,128)(2,1)S(1)}, bf16[128,2048]{1,0:T(8,128)(2,1)S(1)}, u32[]{:S(2)}, u32[]{:S(2)}) collective-permute-start(bf16[128,2048]{1,0:T(8,128)(2,1)S(1)} %get-tuple-element.1276), channel_id=1, source_target_pairs={{32,0},{64,32},{96,64},{128,96},{160,128},{192,160},{224,192},{33,... | collective-permute-start | bytes 1572872 | tf_op jit(solution)/shard_map/while/body/eval_jaxpr/ppermute | solution.py:29
  769.1 24.6 %collective-permute-start.7 = (bf16[128,2048]{1,0:T(8,128)(2,1)S(1)}, bf16[128,2048]{1,0:T(8,128)(2,1)S(1)}, u32[]{:S(2)}, u32[]{:S(2)}) collective-permute-start(bf16[128,2048]{1,0:T(8,128)(2,1)S(1)} %get-tuple-element.1276), channel_id=1, source_target_pairs={{32,0},{64,32},{96,64},{128,96},{160,128},{192,160},{224,192},{33,... | collective-permute-start | bytes 1572872 | tf_op jit(solution)/shard_map/while/body/eval_jaxpr/ppermute | solution.py:29
  870.6 16.0 %collective-permute-start.7 = (bf16[128,2048]{1,0:T(8,128)(2,1)S(1)}, bf16[128,2048]{1,0:T(8,128)(2,1)S(1)}, u32[]{:S(2)}, u32[]{:S(2)}) collective-permute-start(bf16[128,2048]{1,0:T(8,128)(2,1)S(1)} %get-tuple-element.1276), channel_id=1, source_target_pairs={{32,0},{64,32},{96,64},{128,96},{160,128},{192,160},{224,192},{33,... | collective-permute-start | bytes 1572872 | tf_op jit(solution)/shard_map/while/body/eval_jaxpr/ppermute | solution.py:29
  920.3 178.7 %collective-permute-start.7 = (bf16[128,2048]{1,0:T(8,128)(2,1)S(1)}, bf16[128,2048]{1,0:T(8,128)(2,1)S(1)}, u32[]{:S(2)}, u32[]{:S(2)}) collective-permute-start(bf16[128,2048]{1,0:T(8,128)(2,1)S(1)} %get-tuple-element.1276), channel_id=1, source_target_pairs={{32,0},{64,32},{96,64},{128,96},{160,128},{192,160},{224,192},{33,... | collective-permute-start | bytes 1572872 | tf_op jit(solution)/shard_map/while/body/eval_jaxpr/ppermute | solution.py:29
  1161.5 11.5 collective-permute-start.7
  1278.8 29.2 %collective-permute-start.7 = (bf16[128,2048]{1,0:T(8,128)(2,1)S(1)}, bf16[128,2048]{1,0:T(8,128)(2,1)S(1)}, u32[]{:S(2)}, u32[]{:S(2)}) collective-permute-start(bf16[128,2048]{1,0:T(8,128)(2,1)S(1)} %get-tuple-element.1276), channel_id=1, source_target_pairs={{32,0},{64,32},{96,64},{128,96},{160,128},{192,160},{224,192},{33,... | collective-permute-start | bytes 1572872 | tf_op jit(solution)/shard_map/while/body/eval_jaxpr/ppermute | solution.py:29
  (102 other events, 568.7 us)
Sparse Core Ops, SparseCore 0:
  10.6 78.3 all-gather.8
  91.5 79.1 all-gather.10
  173.3 79.1 all-gather.12
  254.9 79.1 all-gather.14
where the time goes:
time: 1320 us
  waiting for transfers between devices  710 us (54%)
  starting transfers between devices  363 us (28%)
  other arithmetic  89.5 us (7%)
  local copies, waits for them, and re-layouts  75.9 us (6%)
  matrix products  59.4 us (4%)
  between operations  13.8 us (1%)
    ppermute x18, waiting for transfers between devices, shifted(): return lax.ppermute(block, axis, route)  301 us
    ppermute x27, starting transfers between devices, padded(): lax.ppermute(lax.slice_in_dim(block, block.shape[dim] - width, None, axis...  191 us
    ppermute x18, starting transfers between devices, shifted(): return lax.ppermute(block, axis, route)  120 us
    select_n x45, other arithmetic, put_slot(): jnp.where(active, lax.dynamic_update_index_in_dim(buffer, value, slot, 0)...  83.1 us
    all_gather x1, waiting for transfers between devices, per_device(): lax.all_gather(w_value[0], 'ctx', axis=0, tiled=True)  81.8 us
    all_gather x1, waiting for transfers between devices, per_device(): lax.all_gather(w_key[0], 'ctx', axis=0, tiled=True)  81.8 us
    all_gather x1, waiting for transfers between devices, per_device(): lax.all_gather(w_out[0], 'ctx', axis=0, tiled=True)  81.6 us
    all_gather x1, waiting for transfers between devices, per_device(): lax.all_gather(w_query[0], 'ctx', axis=0, tiled=True)  78 us
  transfers between devices with their start and end apart: 76, of which 49 were waited for; matrix products, arithmetic and copies ran while one was open for 4% of the time, Pallas kernels for 0%

commit v1 on v0

--- a/solution.py
+++ b/solution.py
@@ -97,9 +97,18 @@
     micro = section_input.shape[0]
     length = section_input.shape[1]
     width = HEADS * HDIM
+
+    def view_vectors(work_x, axis_name, dimension_no):
+        chunks = []
+        for _ in range(lax.axis_size(axis_name)):
+            chunks.append(work_x)
+        return jnp.concatenate(
+            lax.all_to_all(jnp.stack(chunks), axis_name, 0, 0), axis=dimension_no
+        )
+
     full_query, full_key, full_value, full_out = (
         lax.all_gather(w_query[0], "ctx", axis=0, tiled=True),
-        lax.all_gather(w_key[0], "ctx", axis=0, tiled=True),
+        view_vectors(w_key[0], "ctx", 0),
         lax.all_gather(w_value[0], "ctx", axis=0, tiled=True),
         lax.all_gather(w_out[0], "ctx", axis=0, tiled=True),
     )

time: 1320 us -> 1320 us (level)
  starting transfers between devices: 363 us -> 377 us
    all_gather x1 -> x0, waiting for transfers between devices: 81.8 us -> none  [per_device(): lax.all_gather(w_key[0], 'ctx', axis=0, tiled=True)]
    all_gather x1, waiting for transfers between devices: 78 us -> 119 us  [per_device(): lax.all_gather(w_query[0], 'ctx', axis=0, tiled=True)]
    ppermute x18, waiting for transfers between devices: 301 us -> 339 us  [shifted(): return lax.ppermute(block, axis, route)]
    while x54, local copies, waits for them, and re-layouts: 14.1 us -> 0.48 us
  transfers between devices with their start and end apart: 76 -> 76, of which waited for: 49 -> 48; matrix products, arithmetic and copies ran while one was open for 4% -> 3% of each run, Pallas kernels for 0% -> 0%
where the time goes in v1:
time: 1320 us; the launch traced here: 1310 us
  waiting for transfers between devices  702 us (53%)
  starting transfers between devices  377 us (29%)
  other arithmetic  81.4 us (6%)
  local copies, waits for them, and re-layouts  72.3 us (5%)
  matrix products  63.6 us (5%)
  between operations  13.8 us (1%)
    ppermute x18, waiting for transfers between devices, shifted(): return lax.ppermute(block, axis, route)  339 us
    ppermute x27, starting transfers between devices, padded(): lax.ppermute(lax.slice_in_dim(block, block.shape[dim] - width, None, axis...  191 us
    ppermute x18, starting transfers between devices, shifted(): return lax.ppermute(block, axis, route)  125 us
    all_gather x1, waiting for transfers between devices, per_device(): lax.all_gather(w_query[0], 'ctx', axis=0, tiled=True)  119 us
    all_gather x1, waiting for transfers between devices, per_device(): lax.all_gather(w_out[0], 'ctx', axis=0, tiled=True)  81.8 us
    all_gather x1, waiting for transfers between devices, per_device(): lax.all_gather(w_value[0], 'ctx', axis=0, tiled=True)  77.9 us
    select_n x45, other arithmetic, put_slot(): jnp.where(active, lax.dynamic_update_index_in_dim(buffer, value, slot, 0)...  71.4 us
    ppermute x27, waiting for transfers between devices, padded(): lax.ppermute(lax.slice_in_dim(block, 0, width, axis=dim), axis, backward)  68.9 us
  transfers between devices with their start and end apart: 76, of which 48 were waited for; matrix products, arithmetic and copies ran while one was open for 3% of the time, Pallas kernels for 0%

profile of v1, /device:TPU:103, one launch (start us, length us, event | category | flops | bytes accessed | tf_op | source)
XLA Modules:
  0.0 1315.0 jit_solution(4486062442109344808)
XLA Ops:
  12.0 9.8 all-to-all-start
  23.0 118.6 %all-gather.7.cloned.1.call-done = bf16[1,2048,1024]{2,1,0:T(8,128)(2,1)} async-done(((bf16[1,64,1024]{2,1,0:T(8,128)(2,1)}), bf16[1,2048,1024]{2,1,0:T(8,128)(2,1)}) %all-gather.7.cloned.1.call-update) | async-done | bytes 4194320 | tf_op jit(solution)/shard_map/all_gather | solution.py:110
  141.6 77.9 %all-gather.9.cloned.1.call-done = bf16[1,2048,1024]{2,1,0:T(8,128)(2,1)} async-done(((bf16[1,64,1024]{2,1,0:T(8,128)(2,1)}), bf16[1,2048,1024]{2,1,0:T(8,128)(2,1)}) %all-gather.9.cloned.1.call-update) | async-done | bytes 4194320 | tf_op jit(solution)/shard_map/all_gather | solution.py:112
  219.5 81.8 %all-gather.11.cloned.1.call-done = bf16[1,1024,2048]{2,1,0:T(8,128)(2,1)} async-done(((bf16[1,32,2048]{2,1,0:T(8,128)(2,1)}), bf16[1,1024,2048]{2,1,0:T(8,128)(2,1)}) %all-gather.11.cloned.1.call-update) | async-done | bytes 4194320 | tf_op jit(solution)/shard_map/all_gather | solution.py:113
  305.3 306.7 %while.41 = (s32[]{:T(128)}, bf16[128,2048]{1,0:T(8,128)(2,1)}, bf16[2,128,2048]{2,1,0:T(8,128)(2,1)S(1)}, bf16[2,128,2048]{2,1,0:T(8,128)(2,1)}, bf16[2,128,102...) while((s32[]{:T(128)}, bf16[128,2048]{1,0:T(8,128)(2,1)}, ...), condition=%wide.region_9.10_spmd, body=%wide.region_0.9_spmd.sunk | while | flops 2211841024 | bytes 80431864 | solution.py:160
  328.8 14.7 %collective-permute-done.2 = bf16[128,2048]{1,0:T(8,128)(2,1)} collective-permute-done((bf16[128,2048]{1,0:T(8,128)(2,1)}, bf16[128,2048]{1,0:T(8,128)(2,1)}, u32[]{:S(2)}, u32[]{:S(2)}) %collective-permute-start.2) | collective-permute-done | bytes 524320 | tf_op jit(solution)/shard_map/while/body/eval_jaxpr/ppermute | solution.py:29
  345.0 10.8 conditional.8
  384.5 10.8 conditional.8
  439.3 22.2 %collective-permute-start.2 = (bf16[128,2048]{1,0:T(8,128)(2,1)}, bf16[128,2048]{1,0:T(8,128)(2,1)}, u32[]{:S(2)}, u32[]{:S(2)}) collective-permute-start(bf16[128,2048]{1,0:T(8,128)(2,1)} %get-tuple-element.1251), channel_id=1, source_target_pairs={{0,32},{32,64},{64,96},{96,128},{128,160},{160,192},{192,224},{1,3... | collective-permute-start | bytes 1572872 | tf_op jit(solution)/shard_map/while/body/eval_jaxpr/ppermute | solution.py:29
  561.5 18.6 %collective-permute-start.2 = (bf16[128,2048]{1,0:T(8,128)(2,1)}, bf16[128,2048]{1,0:T(8,128)(2,1)}, u32[]{:S(2)}, u32[]{:S(2)}) collective-permute-start(bf16[128,2048]{1,0:T(8,128)(2,1)} %get-tuple-element.1251), channel_id=1, source_target_pairs={{0,32},{32,64},{64,96},{96,128},{128,160},{160,192},{192,224},{1,3... | collective-permute-start | bytes 1572872 | tf_op jit(solution)/shard_map/while/body/eval_jaxpr/ppermute | solution.py:29
  613.2 695.2 %while.42 = (s32[]{:T(128)}, bf16[128,2048]{1,0:T(8,128)(2,1)S(1)}, bf16[2,128,2048]{2,1,0:T(8,128)(2,1)}, s32[]{:T(128)}, bf16[2,2,128,1024]{3,2,1,0:T(8,128)(2...) while((s32[]{:T(128)}, bf16[128,2048]{1,0:T(8,128)(2,1)S(1)}, ...), condition=%wide.region_24.25_spmd, body=%wide.region_10.24_spmd.sunk | while | flops 3389073152 | bytes 146007536 | solution.py:207
  648.1 14.5 %collective-permute-done.7 = bf16[128,2048]{1,0:T(8,128)(2,1)S(1)} collective-permute-done((bf16[128,2048]{1,0:T(8,128)(2,1)S(1)}, bf16[128,2048]{1,0:T(8,128)(2,1)S(1)}, u32[]{:S(2)}, u32[]{:S(2)}) %collective-permute-start.7) | collective-permute-done | bytes 524320 | tf_op jit(solution)/shard_map/while/body/eval_jaxpr/ppermute | solution.py:29
  698.2 8.6 collective-permute-done.7
  740.9 24.7 %collective-permute-done.7 = bf16[128,2048]{1,0:T(8,128)(2,1)S(1)} collective-permute-done((bf16[128,2048]{1,0:T(8,128)(2,1)S(1)}, bf16[128,2048]{1,0:T(8,128)(2,1)S(1)}, u32[]{:S(2)}, u32[]{:S(2)}) %collective-permute-start.7) | collective-permute-done | bytes 524320 | tf_op jit(solution)/shard_map/while/body/eval_jaxpr/ppermute | solution.py:29
  799.7 9.5 collective-permute-done.7
  843.4 16.5 %collective-permute-done.7 = bf16[128,2048]{1,0:T(8,128)(2,1)S(1)} collective-permute-done((bf16[128,2048]{1,0:T(8,128)(2,1)S(1)}, bf16[128,2048]{1,0:T(8,128)(2,1)S(1)}, u32[]{:S(2)}, u32[]{:S(2)}) %collective-permute-start.7) | collective-permute-done | bytes 524320 | tf_op jit(solution)/shard_map/while/body/eval_jaxpr/ppermute | solution.py:29
  894.0 197.5 %collective-permute-done.7 = bf16[128,2048]{1,0:T(8,128)(2,1)S(1)} collective-permute-done((bf16[128,2048]{1,0:T(8,128)(2,1)S(1)}, bf16[128,2048]{1,0:T(8,128)(2,1)S(1)}, u32[]{:S(2)}, u32[]{:S(2)}) %collective-permute-start.7) | collective-permute-done | bytes 524320 | tf_op jit(solution)/shard_map/while/body/eval_jaxpr/ppermute | solution.py:29
  1103.2 11.8 conditional.10
  1132.3 22.2 %conditional.11 = (bf16[128,2048]{1,0:T(8,128)(2,1)S(1)}) conditional(s32[]{:T(128)} %convert_element_type.302, () %tuple.209, (bf16[2,192,1024]{2,1,0:T(8,128)(2,1)S(1)}, bf16[2,32,1024]{2,1,0:T(8,128)(2,1)}, bf16[2,32,1024]{2,1,0:T(8,128)(2,1)}, bf16[2048,1024]{1,0:T(8,128)(2,1)}, bf16[2,128,2048]{2,1,0:T(8,128)(2,1)S(1)}, /*index=5*/s32[]{:T(128)}, ...), branch_computations={%region_15.15_spmd, %region_16.23_spmd} | conditional | flops 2693800704 | bytes 71440024 | solution.py:201
  1158.6 9.5 collective-permute-done.7
  1179.8 11.8 conditional.10
  1208.9 22.2 %conditional.11 = (bf16[128,2048]{1,0:T(8,128)(2,1)S(1)}) conditional(s32[]{:T(128)} %convert_element_type.302, () %tuple.209, (bf16[2,192,1024]{2,1,0:T(8,128)(2,1)S(1)}, bf16[2,32,1024]{2,1,0:T(8,128)(2,1)}, bf16[2,32,1024]{2,1,0:T(8,128)(2,1)}, bf16[2048,1024]{1,0:T(8,128)(2,1)}, bf16[2,128,2048]{2,1,0:T(8,128)(2,1)S(1)}, /*index=5*/s32[]{:T(128)}, ...), branch_computations={%region_15.15_spmd, %region_16.23_spmd} | conditional | flops 2693800704 | bytes 71440024 | solution.py:201
  1235.1 8.6 collective-permute-done.7
  1275.9 31.0 %collective-permute-start.7 = (bf16[128,2048]{1,0:T(8,128)(2,1)S(1)}, bf16[128,2048]{1,0:T(8,128)(2,1)S(1)}, u32[]{:S(2)}, u32[]{:S(2)}) collective-permute-start(bf16[128,2048]{1,0:T(8,128)(2,1)S(1)} %get-tuple-element.1276), channel_id=1, source_target_pairs={{32,0},{64,32},{96,64},{128,96},{160,128},{192,160},{224,192},{33,... | collective-permute-start | bytes 1572872 | tf_op jit(solution)/shard_map/while/body/eval_jaxpr/ppermute | solution.py:29
  (702 shorter events, 661.7 us)
Async XLA Ops:
  7.2 134.4 %all-gather.7.cloned.1.call-start = ((), (), s32[]{:S(2)}) async-start(), calls=%async_computation.1 | async-start | bytes 4325376 | tf_op jit(solution)/shard_map/all_gather | solution.py:110
  7.9 211.6 %all-gather.9.cloned.1.call-start = ((), (), s32[]{:S(2)}) async-start(), calls=%async_computation.2 | async-start | bytes 4325376 | tf_op jit(solution)/shard_map/all_gather | solution.py:112
  12.0 129.6 %all-to-all-start = ((bf16[32,64,1024]{2,1,0:T(8,128)(2,1)}), bf16[32,64,1024]{2,1,0:T(8,128)(2,1)}, u32[]{:S(2)}, u32[]{:S(2)}) async-start(bf16[32,64,1024]{2,1,0:T(8,128)(2,1)} %stack.74), calls=%async_computation | async-start | bytes 8388608 | tf_op jit(solution)/shard_map/all_to_all | solution.py:106
  21.9 279.4 %all-gather.11.cloned.1.call-start = ((), (), s32[]{:S(2)}) async-start(), calls=%async_computation.3 | async-start | bytes 4325376 | tf_op jit(solution)/shard_map/all_gather | solution.py:113
  318.7 24.8 %collective-permute-start.2 = (bf16[128,2048]{1,0:T(8,128)(2,1)}, bf16[128,2048]{1,0:T(8,128)(2,1)}, u32[]{:S(2)}, u32[]{:S(2)}) collective-permute-start(bf16[128,2048]{1,0:T(8,128)(2,1)} %get-tuple-element.1251), channel_id=1, source_target_pairs={{0,32},{32,64},{64,96},{96,128},{128,160},{160,192},{192,224},{1,3... | collective-permute-start | bytes 1572872 | tf_op jit(solution)/shard_map/while/body/eval_jaxpr/ppermute | solution.py:29
  355.9 11.4 collective-permute-start
  413.7 11.5 collective-permute-start.2
  426.9 11.4 collective-permute-start
  439.3 28.6 %collective-permute-start.2 = (bf16[128,2048]{1,0:T(8,128)(2,1)}, bf16[128,2048]{1,0:T(8,128)(2,1)}, u32[]{:S(2)}, u32[]{:S(2)}) collective-permute-start(bf16[128,2048]{1,0:T(8,128)(2,1)} %get-tuple-element.1251), channel_id=1, source_target_pairs={{0,32},{32,64},{64,96},{96,128},{128,160},{160,192},{192,224},{1,3... | collective-permute-start | bytes 1572872 | tf_op jit(solution)/shard_map/while/body/eval_jaxpr/ppermute | solution.py:29
  469.6 11.4 collective-permute-start
  482.0 11.5 collective-permute-start.2
  507.6 14.2 %collective-permute-start.2 = (bf16[128,2048]{1,0:T(8,128)(2,1)}, bf16[128,2048]{1,0:T(8,128)(2,1)}, u32[]{:S(2)}, u32[]{:S(2)}) collective-permute-start(bf16[128,2048]{1,0:T(8,128)(2,1)} %get-tuple-element.1251), channel_id=1, source_target_pairs={{0,32},{32,64},{64,96},{96,128},{128,160},{160,192},{192,224},{1,3... | collective-permute-start | bytes 1572872 | tf_op jit(solution)/shard_map/while/body/eval_jaxpr/ppermute | solution.py:29
  523.5 11.4 collective-permute-start
  535.8 11.5 collective-permute-start.2
  561.5 25.0 %collective-permute-start.2 = (bf16[128,2048]{1,0:T(8,128)(2,1)}, bf16[128,2048]{1,0:T(8,128)(2,1)}, u32[]{:S(2)}, u32[]{:S(2)}) collective-permute-start(bf16[128,2048]{1,0:T(8,128)(2,1)} %get-tuple-element.1251), channel_id=1, source_target_pairs={{0,32},{32,64},{64,96},{96,128},{128,160},{160,192},{192,224},{1,3... | collective-permute-start | bytes 1572872 | tf_op jit(solution)/shard_map/while/body/eval_jaxpr/ppermute | solution.py:29
  588.2 11.4 collective-permute-start
  600.5 11.5 collective-permute-start.2
  646.1 16.4 %collective-permute-start.7 = (bf16[128,2048]{1,0:T(8,128)(2,1)S(1)}, bf16[128,2048]{1,0:T(8,128)(2,1)S(1)}, u32[]{:S(2)}, u32[]{:S(2)}) collective-permute-start(bf16[128,2048]{1,0:T(8,128)(2,1)S(1)} %get-tuple-element.1276), channel_id=1, source_target_pairs={{32,0},{64,32},{96,64},{128,96},{160,128},{192,160},{224,192},{33,... | collective-permute-start | bytes 1572872 | tf_op jit(solution)/shard_map/while/body/eval_jaxpr/ppermute | solution.py:29
  739.0 26.6 %collective-permute-start.7 = (bf16[128,2048]{1,0:T(8,128)(2,1)S(1)}, bf16[128,2048]{1,0:T(8,128)(2,1)S(1)}, u32[]{:S(2)}, u32[]{:S(2)}) collective-permute-start(bf16[128,2048]{1,0:T(8,128)(2,1)S(1)} %get-tuple-element.1276), channel_id=1, source_target_pairs={{32,0},{64,32},{96,64},{128,96},{160,128},{192,160},{224,192},{33,... | collective-permute-start | bytes 1572872 | tf_op jit(solution)/shard_map/while/body/eval_jaxpr/ppermute | solution.py:29
  797.8 11.5 collective-permute-start.7
  841.5 18.5 %collective-permute-start.7 = (bf16[128,2048]{1,0:T(8,128)(2,1)S(1)}, bf16[128,2048]{1,0:T(8,128)(2,1)S(1)}, u32[]{:S(2)}, u32[]{:S(2)}) collective-permute-start(bf16[128,2048]{1,0:T(8,128)(2,1)S(1)} %get-tuple-element.1276), channel_id=1, source_target_pairs={{32,0},{64,32},{96,64},{128,96},{160,128},{192,160},{224,192},{33,... | collective-permute-start | bytes 1572872 | tf_op jit(solution)/shard_map/while/body/eval_jaxpr/ppermute | solution.py:29
  892.1 199.4 %collective-permute-start.7 = (bf16[128,2048]{1,0:T(8,128)(2,1)S(1)}, bf16[128,2048]{1,0:T(8,128)(2,1)S(1)}, u32[]{:S(2)}, u32[]{:S(2)}) collective-permute-start(bf16[128,2048]{1,0:T(8,128)(2,1)S(1)} %get-tuple-element.1276), channel_id=1, source_target_pairs={{32,0},{64,32},{96,64},{128,96},{160,128},{192,160},{224,192},{33,... | collective-permute-start | bytes 1572872 | tf_op jit(solution)/shard_map/while/body/eval_jaxpr/ppermute | solution.py:29
  1156.6 11.5 collective-permute-start.7
  1275.9 32.5 %collective-permute-start.7 = (bf16[128,2048]{1,0:T(8,128)(2,1)S(1)}, bf16[128,2048]{1,0:T(8,128)(2,1)S(1)}, u32[]{:S(2)}, u32[]{:S(2)}) collective-permute-start(bf16[128,2048]{1,0:T(8,128)(2,1)S(1)} %get-tuple-element.1276), channel_id=1, source_target_pairs={{32,0},{64,32},{96,64},{128,96},{160,128},{192,160},{224,192},{33,... | collective-permute-start | bytes 1572872 | tf_op jit(solution)/shard_map/while/body/eval_jaxpr/ppermute | solution.py:29
  (93 other events, 717.7 us)
Sparse Core Ops, SparseCore 0:
  10.6 130.9 all-gather.6
  144.2 75.2 all-gather.8
  222.1 79.1 all-gather.10
